TPU v7x, 32 devices: a whole 2x2x4 slice. The times are simulated.
32 devices in a mesh: row: 8 (over z, core), col: 4 (over y, x).
Axes of the slice: x: 2, y: 2, z: 4, core: 2. Of those that a mesh axis runs over, the one named last changes fastest.
Arguments:
- factor: float32 [10240, 10240], P('row', 'col'), may hold values from -1 to 6, as said below
Outputs:
- progressed: float32 [10240, 10240], P('row', 'col')
Inputs may be any that keep to these rules, and one draw needn't show every extreme that they name: factor is symmetric positive definite with smallest eigenvalue at least 0.5, stored in the block-cyclic order of the steps.
All inputs are finite; a program needn't handle non-finite values.
Results may differ from a plain program's by a relative error of at most 0.0001.
Values sent between devices are 32-bit elements; how exact they have to be, the bound alone decides.
A program may use at most 128 MiB of HBM per device.

v0:
```python
import jax
import jax.numpy as jnp
from jax import lax
from jax.sharding import PartitionSpec as P

TILE = 128
PIVOT = 512
STEPS = 2


def broadcast(value, axis, source):
    kept = jnp.where(lax.axis_index(axis) == source, value, 0).astype(value.dtype)
    return lax.psum(kept, axis)


def per_device(factor):
    rows_count = lax.axis_size("row")
    cols_count = lax.axis_size("col")
    local_rows, local_cols = factor.shape
    row_place = lax.axis_index("row")
    col_place = lax.axis_index("col")
    per_block = PIVOT // TILE
    row_offsets = jnp.arange(local_rows, dtype=jnp.int32)
    row_global = (row_offsets // TILE * rows_count + row_place) * TILE + row_offsets % TILE
    pivot_range = jnp.arange(PIVOT, dtype=jnp.int32)
    identity = jnp.eye(PIVOT, dtype=jnp.float32)

    def gather_columns(slab_of, step):
        slabs = []
        for member in range(per_block):
            tile_no = step * per_block + member
            slabs.append(broadcast(slab_of(tile_no), "col", tile_no % cols_count))
        return jnp.concatenate(slabs, axis=1)

    def plain_slab(matrix):

        def taker(tile_no):
            first = tile_no // cols_count * TILE
            return matrix[:, first : first + TILE]

        return taker

    matrix = factor
    column_panel = gather_columns(plain_slab(matrix), 0)
    for step in range(STEPS):
        row_parts = []
        block_parts = []
        for prepare_member in range(per_block):
            prepare_tile_no = step * per_block + prepare_member
            prepare_first = prepare_tile_no // rows_count * TILE
            got_rows, got_block = (
                broadcast(
                    matrix[prepare_first : prepare_first + TILE, :],
                    "row",
                    prepare_tile_no % rows_count,
                ),
                broadcast(
                    column_panel[prepare_first : prepare_first + TILE, :],
                    "row",
                    prepare_tile_no % rows_count,
                ),
            )
            row_parts.append(got_rows)
            block_parts.append(got_block)
        pivot_rows = jnp.concatenate(row_parts, axis=0)
        pivot_block = jnp.concatenate(block_parts, axis=0)
        lower = jnp.linalg.cholesky(pivot_block)
        prepare_inverse = jax.scipy.linalg.cho_solve((lower, True), identity)
        prepare_scaled = jnp.dot(
            prepare_inverse,
            pivot_rows,
            precision=lax.Precision.HIGHEST,
            preferred_element_type=jnp.float32,
        )
        prepare_marks = (row_global[:, None] - step * PIVOT == pivot_range[None, :]).astype(
            jnp.float32
        )
        prepare_reduced = column_panel - prepare_marks
        prepared = (prepare_inverse, prepare_scaled, prepare_marks, prepare_reduced)
        if step + 1 < STEPS:
            scaled_now = prepared[1]
            reduced_now = prepared[3]

            def early_slab(tile_no, source=matrix, scaled_now=scaled_now, reduced_now=reduced_now):
                first = tile_no // cols_count * TILE
                return source[:, first : first + TILE] - jnp.dot(
                    reduced_now,
                    scaled_now[:, first : first + TILE],
                    precision=lax.Precision.HIGHEST,
                    preferred_element_type=jnp.float32,
                )

            next_panel = gather_columns(early_slab, step + 1)
        inverse, scaled, marks, reduced = prepared
        updated = matrix - jnp.dot(
            reduced, scaled, precision=lax.Precision.HIGHEST, preferred_element_type=jnp.float32
        )
        fixed = marks - jnp.dot(
            reduced, inverse, precision=lax.Precision.HIGHEST, preferred_element_type=jnp.float32
        )
        for finish_member in range(per_block):
            finish_tile_no = step * per_block + finish_member
            finish_first = finish_tile_no // cols_count * TILE
            current = updated[:, finish_first : finish_first + TILE]
            chosen = jnp.where(
                col_place == finish_tile_no % cols_count,
                fixed[:, finish_member * TILE : (finish_member + 1) * TILE],
                current,
            )
            updated = updated.at[:, finish_first : finish_first + TILE].set(chosen)
        matrix = updated
        if step + 1 < STEPS:
            column_panel = next_panel
    return matrix


def solution(mesh):
    placed = (P("row", "col"),)
    return jax.shard_map(
        per_device, mesh=mesh, in_specs=placed, out_specs=P("row", "col"), check_vma=False
    )
```

profile of v0, /device:TPU:13, one launch (start us, length us, event | category | flops | bytes accessed | tf_op | source)
XLA Modules:
  0.0 921.7 jit_solution(14794230671533546266)
XLA Ops:
  6.5 13.9 %copy.5 = f32[1280,2560]{0,1:T(8,128)} copy(f32[1280,2560]{1,0:T(8,128)} %param.20) | data formatting | bytes 26214400 | tf_op args[0]
  20.4 2.6 slice_select_fusion.8
  23.1 3.8 slice_select_fusion.7
  26.9 75.4 %all-reduce.16.cloned.1.call-done = (f32[1280,128]{0,1:T(8,128)}, f32[1280,128]{0,1:T(8,128)}, f32[1280,128]{0,1:T(8,128)}, f32[1280,128]{0,1:T(8,128)}) async-done(((f32[1280,128]{0,1:T(8,128)}, f32[1280,128]{0,1:T(8,128)}, f32[1280,128]{0,1:T(8,128)}, f32[1280,128]{0,1:T(8,128)}), (f32[1280,128]{0,1:T(8,128)}, f32[1280,128]{0,1:T(8,128)}, f32[1280,128]{0,1:T(8,128)}, ...) | async-done | bytes 2621456 | tf_op jit(solution)/shard_map/psum | solution.py:13
  107.7 134.4 %all-reduce.12.cloned.1.call-done = (f32[128,2560]{0,1:T(8,128)}, f32[128,2560]{0,1:T(8,128)}, f32[128,2560]{0,1:T(8,128)}, f32[128,2560]{0,1:T(8,128)}, f32[128...) async-done(((f32[128,2560]{0,1:T(8,128)}, f32[128,2560]{0,1:T(8,128)}, f32[128,2560]{0,1:T(8,128)}, f32[128,2560]{0,1:T(8,128)}, ...) | async-done | bytes 6291472 | tf_op jit(solution)/shard_map/psum | solution.py:13
  248.9 2.6 copy.3
  254.3 11.7 %cholesky.286 = f32[128,128]{1,0:T(8,128)S(1)} custom-call(f32[128,128]{1,0:T(8,128)S(1)} %cholesky.426), custom_call_target="Cholesky" | custom-call | tf_op jit(solution)/shard_map/jit(cholesky)/cholesky | solution.py:67
  266.0 9.8 %custom-call.29 = f32[1,128,128]{1,2,0:T(8,128)S(1)} custom-call(f32[1,128,128]{2,1,0:T(8,128)S(1)} %get-tuple-element.214), custom_call_target="InvertDiagBlocksLowerTriangular" | custom-call | tf_op jit(solution)/shard_map/jit(cholesky)/cholesky | solution.py:67
  280.2 11.7 %cholesky.305 = f32[128,128]{1,0:T(8,128)S(1)} custom-call(f32[128,128]{1,0:T(8,128)S(1)} %cholesky.430), custom_call_target="Cholesky" | custom-call | tf_op jit(solution)/shard_map/jit(cholesky)/cholesky | solution.py:67
  292.5 10.0 %custom-call.30 = f32[1,128,128]{1,2,0:T(8,128)S(1)} custom-call(f32[1,128,128]{2,1,0:T(8,128)S(1)} %get-tuple-element.211), custom_call_target="InvertDiagBlocksLowerTriangular" | custom-call | tf_op jit(solution)/shard_map/jit(cholesky)/cholesky | solution.py:67
  304.9 11.7 %cholesky.326 = f32[128,128]{1,0:T(8,128)S(1)} custom-call(f32[128,128]{1,0:T(8,128)S(1)} %cholesky.435), custom_call_target="Cholesky" | custom-call | tf_op jit(solution)/shard_map/jit(cholesky)/cholesky | solution.py:67
  317.9 9.8 %custom-call.31 = f32[1,128,128]{1,2,0:T(8,128)S(1)} custom-call(f32[1,128,128]{2,1,0:T(8,128)S(1)} %get-tuple-element.208), custom_call_target="InvertDiagBlocksLowerTriangular" | custom-call | tf_op jit(solution)/shard_map/jit(cholesky)/cholesky | solution.py:67
  330.0 22.1 %cholesky.343 = f32[128,128]{1,0:T(8,128)S(1)} custom-call(f32[128,128]{1,0:T(8,128)S(1)} %convolution_subtract_fusion.20), custom_call_target="Cholesky" | custom-call | tf_op jit(solution)/shard_map/jit(cholesky)/cholesky | solution.py:67
  356.5 2.3 select_select_fusion.1
  358.9 11.7 %while.12 = (s32[]{:T(128)}, f32[512,512]{1,0:T(8,128)}, s32[4,2]{0,1:T(2,128)S(1)}, f32[4,128,128]{2,1,0:T(8,128)S(1)}, s32[]{:T(128)}) while((s32[]{:T(128)}, f32[512,512]{1,0:T(8,128)}, s32[4,2]{0,1:T(2,128)S(1)}, f32[4,128,128]{2,1,0:T(8,128)S(1)}, s32[]{:T(128)}) %tuple.105), condition=%wide.while_cond.8, body=%wide.while_body.8.sunk | while | flops 2 | bytes 131189 | solution.py:68
  359.6 2.3 bitcast_dynamic-update-slice_fusion.4
  362.5 2.3 bitcast_dynamic-update-slice_fusion.4
  365.5 2.3 bitcast_dynamic-update-slice_fusion.4
  368.4 2.2 bitcast_dynamic-update-slice_fusion.4
  370.6 39.3 %custom-call.32 = f32[4,128,128]{1,2,0:T(8,128)S(1)} custom-call(f32[4,128,128]{2,1,0:T(8,128)S(1)} %get-tuple-element.117), custom_call_target="InvertDiagBlocksLowerTriangular" | custom-call | tf_op jit(solution)/shard_map/jit(_cho_solve)/triangular_solve | solution.py:68
  420.4 6.2 convert_subtract_fusion.2
  426.6 9.2 fusion
  435.9 3.6 broadcast_select_fusion
  439.5 26.3 %convolution_subtract_fusion.1 = f32[1280,2560]{0,1:T(8,128)} fusion(f32[1280,2560]{0,1:T(8,128)S(1)} %bitcast.117, f32[512,2560]{1,0:T(8,128)S(1)} %fusion, f32[1280,512]{0,1:T(8,128)S(1)} %constant_dynamic-update-slice_fusion, s32[1280]{0:T(1024)S(1)} %fusion.122), kind=kOutput, calls=%fused_computation.5 | convolution fusion | flops 20137902080 | bytes 34083840 | tf_op jit(solution)/shard_map/dot_general | solution.py:95
  467.5 2.6 constant_dynamic-update-slice_fusion.23
  474.6 3.8 slice_select_fusion.3
  478.4 66.0 %all-reduce.14.cloned.1.call-done = (f32[1280,128]{0,1:T(8,128)}, f32[1280,128]{0,1:T(8,128)}, f32[1280,128]{0,1:T(8,128)}, f32[1280,128]{0,1:T(8,128)}) async-done(((f32[1280,128]{0,1:T(8,128)}, f32[1280,128]{0,1:T(8,128)}, f32[1280,128]{0,1:T(8,128)}, f32[1280,128]{0,1:T(8,128)}), (f32[1280,128]{0,1:T(8,128)}, f32[1280,128]{0,1:T(8,128)}, f32[1280,128]{0,1:T(8,128)}, ...) | async-done | bytes 2621456 | tf_op jit(solution)/shard_map/psum | solution.py:13
  548.8 135.4 %all-reduce.10.cloned.1.call-done = (f32[128,2560]{0,1:T(8,128)}, f32[128,2560]{0,1:T(8,128)}, f32[128,2560]{0,1:T(8,128)}, f32[128,2560]{0,1:T(8,128)}, f32[128...) async-done(((f32[128,2560]{0,1:T(8,128)}, f32[128,2560]{0,1:T(8,128)}, f32[128,2560]{0,1:T(8,128)}, f32[128,2560]{0,1:T(8,128)}, ...) | async-done | bytes 6291472 | tf_op jit(solution)/shard_map/psum | solution.py:13
  691.1 2.5 copy.10
  696.4 11.7 %cholesky.358 = f32[128,128]{1,0:T(8,128)S(1)} custom-call(f32[128,128]{1,0:T(8,128)S(1)} %cholesky.439), custom_call_target="Cholesky" | custom-call | tf_op jit(solution)/shard_map/jit(cholesky)/cholesky | solution.py:67
  708.8 9.8 %custom-call.33 = f32[1,128,128]{1,2,0:T(8,128)S(1)} custom-call(f32[1,128,128]{2,1,0:T(8,128)S(1)} %get-tuple-element.204), custom_call_target="InvertDiagBlocksLowerTriangular" | custom-call | tf_op jit(solution)/shard_map/jit(cholesky)/cholesky | solution.py:67
  722.9 11.7 %cholesky.377 = f32[128,128]{1,0:T(8,128)S(1)} custom-call(f32[128,128]{1,0:T(8,128)S(1)} %cholesky.443), custom_call_target="Cholesky" | custom-call | tf_op jit(solution)/shard_map/jit(cholesky)/cholesky | solution.py:67
  736.0 10.2 %custom-call.34 = f32[1,128,128]{1,2,0:T(8,128)S(1)} custom-call(f32[1,128,128]{2,1,0:T(8,128)S(1)} %get-tuple-element.201), custom_call_target="InvertDiagBlocksLowerTriangular" | custom-call | tf_op jit(solution)/shard_map/jit(cholesky)/cholesky | solution.py:67
  748.6 11.7 %cholesky.398 = f32[128,128]{1,0:T(8,128)S(1)} custom-call(f32[128,128]{1,0:T(8,128)S(1)} %cholesky.448), custom_call_target="Cholesky" | custom-call | tf_op jit(solution)/shard_map/jit(cholesky)/cholesky | solution.py:67
  761.6 9.8 %custom-call.35 = f32[1,128,128]{1,2,0:T(8,128)S(1)} custom-call(f32[1,128,128]{2,1,0:T(8,128)S(1)} %get-tuple-element.198), custom_call_target="InvertDiagBlocksLowerTriangular" | custom-call | tf_op jit(solution)/shard_map/jit(cholesky)/cholesky | solution.py:67
  773.6 11.9 %cholesky.415 = f32[128,128]{1,0:T(8,128)S(1)} custom-call(f32[128,128]{1,0:T(8,128)S(1)} %convolution_subtract_fusion.19), custom_call_target="Cholesky" | custom-call | tf_op jit(solution)/shard_map/jit(cholesky)/cholesky | solution.py:67
  789.1 2.4 select_select_fusion
  791.5 11.7 %while.13 = (s32[]{:T(128)}, f32[512,512]{1,0:T(8,128)}, s32[4,2]{0,1:T(2,128)S(1)}, f32[4,128,128]{2,1,0:T(8,128)S(1)}, s32[]{:T(128)}) while((s32[]{:T(128)}, f32[512,512]{1,0:T(8,128)}, s32[4,2]{0,1:T(2,128)S(1)}, f32[4,128,128]{2,1,0:T(8,128)S(1)}, s32[]{:T(128)}) %tuple.123), condition=%wide.while_cond.8.clone, body=%wide.while_body.8.clone.sunk | while | flops 2 | bytes 131189 | solution.py:68
  792.2 2.3 bitcast_dynamic-update-slice_fusion.5
  795.1 2.3 bitcast_dynamic-update-slice_fusion.5
  798.1 2.3 bitcast_dynamic-update-slice_fusion.5
  801.0 2.2 bitcast_dynamic-update-slice_fusion.5
  803.2 39.3 %custom-call.36 = f32[4,128,128]{1,2,0:T(8,128)S(1)} custom-call(f32[4,128,128]{2,1,0:T(8,128)S(1)} %get-tuple-element.118), custom_call_target="InvertDiagBlocksLowerTriangular" | custom-call | tf_op jit(solution)/shard_map/jit(_cho_solve)/triangular_solve | solution.py:68
  853.0 5.0 convert_subtract_fusion
  858.0 9.2 fusion.8
  867.3 25.8 %convolution_subtract_fusion = f32[1280,2560]{0,1:T(8,128)} fusion(f32[1280,2560]{0,1:T(8,128)S(1)} %bitcast.119, f32[512,2560]{1,0:T(8,128)S(1)} %fusion.8, f32[1280,512]{0,1:T(8,128)S(1)} %constant_dynamic-update-slice_fusion.8, s32[1280]{0:T(1024)S(1)} %broadcast_add_fusion), kind=kOutput, calls=%fused_computation.4 | convolution fusion | flops 20137902080 | bytes 34083840 | tf_op jit(solution)/shard_map/dot_general | solution.py:95
  893.1 2.8 constant_dynamic-update-slice_fusion.21
  900.9 13.9 %copy.13 = f32[1280,2560]{1,0:T(8,128)} copy(f32[1280,2560]{0,1:T(8,128)} %fusion.45) | data formatting | bytes 26214400 | tf_op jit(solution)/shard_map/scatter | solution.py:110
  (174 shorter events, 92.6 us)
Async XLA Ops:
  6.5 95.7 %all-reduce.16.cloned.1.call-start = ((), (), s32[]{:S(2)}) async-start(), calls=%async_computation.3 | async-start | bytes 5242880 | tf_op jit(solution)/shard_map/psum | solution.py:13
  23.1 219.1 %all-reduce.12.cloned.1.call-start = ((), (), s32[]{:S(2)}) async-start(), calls=%async_computation.1 | async-start | bytes 12582912 | tf_op jit(solution)/shard_map/psum | solution.py:13
  102.3 2.4 copy-start.8
  102.3 2.4 copy-start.7
  105.9 438.5 %all-reduce.14.cloned.1.call-start = ((), (), s32[]{:S(2)}) async-start(), calls=%async_computation.2 | async-start | bytes 5242880 | tf_op jit(solution)/shard_map/psum | solution.py:13
  253.3 1.0 copy-start.4
  409.9 5.3 copy-start.2
  413.2 22.6 %slice-start = ((s8[13107200]{0:T(1024)(128)(4,1)}), s8[4194304]{0:T(1024)(128)(4,1)S(1)}, s32[]{:S(2)}) async-start(s8[13107200]{0:T(1024)(128)(4,1)} %bitcast.116), calls=%async_computation.4 | async-start | bytes 8388608
  418.4 8.2 copy-start.12
  418.9 16.9 %slice-start.1 = ((s8[13107200]{0:T(1024)(128)(4,1)}), s8[4194304]{0:T(1024)(128)(4,1)S(1)}, s32[]{:S(2)}) async-start(s8[13107200]{0:T(1024)(128)(4,1)} %bitcast.116), calls=%async_computation.5 | async-start | bytes 8388608
  420.0 6.7 copy-start.9
  420.0 6.7 copy-start.10
  420.0 6.6 copy-start.11
  420.4 15.5 %slice-start.2 = ((s8[13107200]{0:T(1024)(128)(4,1)}), s8[4194304]{0:T(1024)(128)(4,1)S(1)}, s32[]{:S(2)}) async-start(s8[13107200]{0:T(1024)(128)(4,1)} %bitcast.116), calls=%async_computation.6 | async-start | bytes 8388608
  426.6 9.2 %slice-start.3 = ((s8[13107200]{0:T(1024)(128)(4,1)}), s8[524288]{0:T(1024)(128)(4,1)S(1)}, s32[]{:S(2)}) async-start(s8[13107200]{0:T(1024)(128)(4,1)} %bitcast.116), calls=%async_computation.7 | async-start | bytes 1048576
  465.8 1.7 copy-start
  465.8 218.4 %all-reduce.10.cloned.1.call-start = ((), (), s32[]{:S(2)}) async-start(), calls=%async_computation | async-start | bytes 12582912 | tf_op jit(solution)/shard_map/psum | solution.py:13
  544.3 2.4 copy-start.6
  544.3 2.4 copy-start.5
  695.4 1.0 copy-start.3
  842.5 5.3 copy-start.1
  845.8 21.4 %slice-start.4 = ((s8[13107200]{0:T(1024)(128)(4,1)}), s8[4194304]{0:T(1024)(128)(4,1)S(1)}, s32[]{:S(2)}) async-start(s8[13107200]{0:T(1024)(128)(4,1)} %bitcast.118), calls=%async_computation.8 | async-start | bytes 8388608
  851.0 7.0 copy-start.16
  851.5 15.7 %slice-start.5 = ((s8[13107200]{0:T(1024)(128)(4,1)}), s8[4194304]{0:T(1024)(128)(4,1)S(1)}, s32[]{:S(2)}) async-start(s8[13107200]{0:T(1024)(128)(4,1)} %bitcast.118), calls=%async_computation.9 | async-start | bytes 8388608
  852.6 5.4 copy-start.13
  852.6 5.4 copy-start.14
  852.6 5.4 copy-start.15
  853.0 14.3 %slice-start.6 = ((s8[13107200]{0:T(1024)(128)(4,1)}), s8[4194304]{0:T(1024)(128)(4,1)S(1)}, s32[]{:S(2)}) async-start(s8[13107200]{0:T(1024)(128)(4,1)} %bitcast.118), calls=%async_computation.10 | async-start | bytes 8388608
  858.0 9.2 %slice-start.7 = ((s8[13107200]{0:T(1024)(128)(4,1)}), s8[524288]{0:T(1024)(128)(4,1)S(1)}, s32[]{:S(2)}) async-start(s8[13107200]{0:T(1024)(128)(4,1)} %bitcast.118), calls=%async_computation.11 | async-start | bytes 1048576
Sparse Core Ops, SparseCore 0:
  23.2 79.0 all-reduce.15
  106.0 136.1 all-reduce.11
  465.9 78.3 all-reduce.13
  548.0 136.1 all-reduce.9
where the time goes:
time: 935 us; the launch traced here: 922 us
  waiting for transfers between devices  411 us (44%)
  other arithmetic  289 us (31%)
  matrix products  121 us (13%)
  local copies, waits for them, and re-layouts  80.7 us (9%)
  between operations  19.2 us (2%)
    psum x4, waiting for transfers between devices, broadcast(): return lax.psum(kept, axis)  411 us
    another operation x29, other arithmetic, per_device(): lower = jnp.linalg.cholesky(pivot_block)  172 us
    another operation x5, other arithmetic, per_device(): prepare_inverse = jax.scipy.linalg.cho_solve((lower, True), identity)  83.3 us
    dot_general x2, matrix products, per_device(): jnp.dot(reduced, scaled, precision=lax.Precision.HIGHEST, preferred_eleme...  52.1 us
    unnamed x63, local copies, waits for them, and re-layouts  32.7 us
    another operation x27, local copies, waits for them, and re-layouts, per_device(): prepare_inverse = jax.scipy.linalg.cho_solve((lower, True), identity)  23.3 us
    another operation x28, matrix products, per_device(): prepare_inverse = jax.scipy.linalg.cho_solve((lower, True), identity)  20.5 us
  transfers between devices with their start and end apart: 4, of which 4 were waited for; matrix products, arithmetic and copies ran while one was open for 2% of the time, Pallas kernels for 0%

commit v1 on v0

v1 whole, which is shorter than its diff:
```python
import jax
import jax.numpy as jnp
from jax import lax
from jax.experimental import pallas as pl
from jax.experimental.pallas import tpu as pltpu
from jax.sharding import PartitionSpec as P

TILE = 128
PIVOT = 512
STEPS = 2
ALL = PIVOT * STEPS
SUB = 8
HIGHEST = lax.Precision.HIGHEST


def dot32(a, b):
    return jnp.dot(a, b, precision=HIGHEST, preferred_element_type=jnp.float32)


def invert_tile(tile):
    groups = TILE // SUB
    strips = [tile[g * SUB : (g + 1) * SUB, :] for g in range(groups)]
    shape = (SUB, TILE)
    lane = lax.broadcasted_iota(jnp.int32, shape, 1)
    sub = lax.broadcasted_iota(jnp.int32, shape, 0)

    def lanes(value, column):
        return jnp.broadcast_to(value[:, column : column + 1], shape)

    def subs(value, row):
        return jnp.broadcast_to(value[row : row + 1, :], shape)

    for g in range(groups):
        first = g * SUB
        panel = strips[g]
        columns = [lanes(panel, first + m) for m in range(SUB)]
        in_group = (lane >= first) & (lane < first + SUB)
        panel = jnp.where(in_group, jnp.where(lane - first == sub, 1.0, 0.0), panel)
        for m in range(SUB):
            own = sub == m
            scale = 1.0 / subs(columns[m], m)
            factor = jnp.where(own, 0.0, columns[m])
            row = subs(panel, m) * scale
            panel = jnp.where(own, row, panel - factor * row)
            for n in range(m + 1, SUB):
                there = subs(columns[n], m) * scale
                columns[n] = jnp.where(own, there, columns[n] - factor * there)
        strips[g] = panel
        rows = [subs(panel, m) for m in range(SUB)]
        for i in range(groups):
            if i == g:
                continue
            value = strips[i]
            total = jnp.where(in_group, 0.0, value)
            for m in range(SUB):
                total = total - lanes(value, first + m) * rows[m]
            strips[i] = total
    return jnp.concatenate(strips, axis=0)


def inverse_kernel(block_ref, out_ref, row_ref, col_ref):
    size = block_ref.shape[0]
    chunk = 2 * TILE
    out_ref[...] = block_ref[...]

    def step(t, carry):
        at = pl.ds(pl.multiple_of(t * TILE, TILE), TILE)
        inverse = invert_tile(out_ref[at, at])
        row_ref[...] = dot32(inverse, out_ref[at, :])
        row_ref[:, at] = inverse
        col_ref[...] = out_ref[:, at]
        out_ref[:, at] = jnp.zeros((size, TILE), jnp.float32)
        for c in range(size // chunk):
            rows = pl.ds(c * chunk, chunk)
            out_ref[rows, :] = out_ref[rows, :] - dot32(col_ref[rows, :], row_ref[...])
        out_ref[at, :] = row_ref[...]
        return carry

    lax.fori_loop(0, size // TILE, step, 0)


def spd_inverse(block):
    size = block.shape[0]
    return pl.pallas_call(
        inverse_kernel,
        out_shape=jax.ShapeDtypeStruct((size, size), jnp.float32),
        in_specs=[pl.BlockSpec(memory_space=pltpu.VMEM)],
        out_specs=pl.BlockSpec(memory_space=pltpu.VMEM),
        scratch_shapes=[
            pltpu.VMEM((TILE, size), jnp.float32),
            pltpu.VMEM((size, TILE), jnp.float32),
        ],
        compiler_params=pltpu.CompilerParams(vmem_limit_bytes=32 << 20),
        cost_estimate=pl.CostEstimate(
            flops=60 * size**3, bytes_accessed=8 * size * size, transcendentals=0
        ),
    )(block)


def per_device(factor):
    rows_count = lax.axis_size("row")
    cols_count = lax.axis_size("col")
    local_rows, local_cols = factor.shape
    row_place = lax.axis_index("row")
    col_place = lax.axis_index("col")
    tiles = ALL // TILE
    row_slots = -(-tiles // rows_count)
    col_slots = -(-tiles // cols_count)
    row_offsets = jnp.arange(local_rows, dtype=jnp.int32)
    row_global = (row_offsets // TILE * rows_count + row_place) * TILE + row_offsets % TILE
    col_offsets = jnp.arange(local_cols, dtype=jnp.int32)
    col_global = (col_offsets // TILE * cols_count + col_place) * TILE + col_offsets % TILE
    pivots = jnp.arange(ALL, dtype=jnp.int32)

    def gather_rows(value):
        width = value.shape[1]
        got = lax.all_gather(value, "row").reshape(rows_count, row_slots, TILE, width)
        return got.transpose(1, 0, 2, 3).reshape(-1, width)[:ALL]

    def gather_cols(value):
        height = value.shape[0]
        got = lax.all_gather(value, "col").reshape(cols_count, height, col_slots, TILE)
        return got.transpose(1, 2, 0, 3).reshape(height, -1)[:, :ALL]

    row_slab = factor[: row_slots * TILE, :]
    col_slab = factor[:, : col_slots * TILE]
    pivot_block = gather_cols(gather_rows(factor[: row_slots * TILE, : col_slots * TILE]))
    pivot_block, row_slab, col_slab = lax.optimization_barrier((pivot_block, row_slab, col_slab))
    pivot_rows = gather_rows(row_slab)
    pivot_cols = gather_cols(col_slab)
    inverse = spd_inverse(pivot_block)

    row_is = row_global < ALL
    col_is = col_global < ALL
    gain = jnp.dot(
        pivot_cols, inverse, precision=lax.Precision.HIGH, preferred_element_type=jnp.float32
    )
    height = row_slots * TILE
    own = jnp.minimum(row_global[:height], ALL - 1).reshape(row_slots, TILE)[:, 0]
    own_inverse = jnp.concatenate(
        [lax.dynamic_slice(inverse, (own[s], 0), (TILE, ALL)) for s in range(row_slots)], axis=0
    )
    head = jnp.where(row_is[:height, None], -own_inverse, gain[:height])
    gain = gain.at[:height].set(head)
    width = col_slots * TILE
    marks = (pivots[:, None] == col_global[None, :width]).astype(jnp.float32)
    lead = jnp.where(col_is[None, :width], marks, pivot_rows[:, :width])
    pivot_rows = pivot_rows.at[:, :width].set(lead)
    base = jnp.where(row_is[:, None] | col_is[None, :], 0.0, factor)
    return base - jnp.dot(
        gain, pivot_rows, precision=lax.Precision.HIGH, preferred_element_type=jnp.float32
    )


def solution(mesh):
    placed = (P("row", "col"),)
    return jax.shard_map(
        per_device, mesh=mesh, in_specs=placed, out_specs=P("row", "col"), check_vma=False
    )
```

time: 935 us -> 306 us (0.33)
  waiting for transfers between devices: 411 us -> 118 us
  other arithmetic: 289 us -> 5.86 us
  matrix products: 121 us -> 41 us
  Pallas kernels: 0 us -> 78.4 us
  local copies, waits for them, and re-layouts: 80.7 us -> 45.3 us
    psum x4 -> x0, waiting for transfers between devices: 411 us -> none  [broadcast(): return lax.psum(kept, axis)]
    another operation x36 -> x1, other arithmetic: 257 us -> 0.65 us  [the longest x29 172 us: per_device(): lower = jnp.linalg.cholesky(pivot_block)]
    all_gather x0 -> x4, waiting for transfers between devices: none -> 117 us  [the longest x2 69 us: gather_rows(): lax.all_gather(value, 'row').reshape(rows_count, row_slots, TILE, width)]
    pallas_call x0 -> x1, Pallas kernels: none -> 78.4 us  [spd_inverse(): pl.pallas_call(inverse_kernel, out_shape=jax.ShapeDtypeStruct((size, size...]
    dot_general x7 -> x2, matrix products: 85.3 us -> 41 us  [the longest x1 27.6 us: per_device(): jnp.dot(gain, pivot_rows, precision=lax.Precision.HIGH, preferred_element...]
    another operation x40 -> x0, matrix products: 36.1 us -> none  [the longest x28 20.5 us: per_device(): prepare_inverse = jax.scipy.linalg.cho_solve((lower, True), identity)]
    unnamed x63 -> x6, local copies, waits for them, and re-layouts: 32.7 us -> 4.15 us
    reshape x0 -> x4, local copies, waits for them, and re-layouts: none -> 25.8 us  [the longest x3 20.3 us: gather_cols(): lax.all_gather(value, 'col').reshape(cols_count, height, col_slots, TILE)]
  transfers between devices with their start and end apart: 4 -> 4, of which waited for: 4 -> 3; matrix products, arithmetic and copies ran while one was open for 2% -> 13% of each run, Pallas kernels for 0% -> 26%
where the time goes in v1:
time: 306 us; the launch traced here: 302 us
  waiting for transfers between devices  118 us (39%)
  Pallas kernels  78.4 us (26%)
  local copies, waits for them, and re-layouts  45.3 us (15%)
  matrix products  41 us (13%)
  between operations  13.3 us (4%)
  other arithmetic  5.86 us (2%)
    pallas_call x1, Pallas kernels, spd_inverse(): pl.pallas_call(inverse_kernel, out_shape=jax.ShapeDtypeStruct((size, size...  78.4 us
    all_gather x2, waiting for transfers between devices, gather_rows(): lax.all_gather(value, 'row').reshape(rows_count, row_slots, TILE, width)  69 us
    all_gather x2, waiting for transfers between devices, gather_cols(): lax.all_gather(value, 'col').reshape(cols_count, height, col_slots, TILE)  48.3 us
    dot_general x1, matrix products, per_device(): jnp.dot(gain, pivot_rows, precision=lax.Precision.HIGH, preferred_element...  27.6 us
    reshape x3, local copies, waits for them, and re-layouts, gather_cols(): lax.all_gather(value, 'col').reshape(cols_count, height, col_slots, TILE)  20.3 us
    dot_general x1, matrix products, per_device(): jnp.dot(pivot_cols, inverse, precision=lax.Precision.HIGH, preferred_elem...  13.3 us
    transpose x1, local copies, waits for them, and re-layouts, gather_cols(): return got.transpose(1, 2, 0, 3).reshape(height, -1)[:, :ALL]  8.82 us
  transfers between devices with their start and end apart: 4, of which 3 were waited for; matrix products, arithmetic and copies ran while one was open for 13% of the time, Pallas kernels for 26%

profile of v1, /device:TPU:13, one launch (start us, length us, event | category | flops | bytes accessed | tf_op | source)
XLA Modules:
  0.0 301.9 jit_solution(9382961158470527494)
XLA Ops:
  6.5 0.0 all-gather.9.cloned.1.call-start
  6.5 1.6 slice.64
  8.1 0.0 all-gather.9.cloned.1.call-update
  8.1 0.0 all-gather.15.cloned.1.call-start
  8.2 24.6 %all-gather.9.cloned.1.call-done = f32[1024,256]{1,0:T(8,128)} async-done(((f32[128,256]{1,0:T(8,128)}), f32[1024,256]{1,0:T(8,128)}) %all-gather.9.cloned.1.call-update) | async-done | bytes 1048592 | tf_op jit(solution)/shard_map/all_gather | solution.py:117
  32.8 0.0 all-gather.15.cloned.1.call-update
  32.8 0.0 all-gather.11.cloned.1.call-start
  32.9 2.6 slice.65
  35.4 2.5 slice.66
  37.9 48.3 %all-gather.15.cloned.1.call-done = f32[4096,256]{1,0:T(8,128)} async-done(((f32[1024,256]{1,0:T(8,128)}), f32[4096,256]{1,0:T(8,128)}) %all-gather.15.cloned.1.call-update) | async-done | bytes 4194320 | tf_op jit(solution)/shard_map/all_gather | solution.py:122
  86.2 5.7 %reshape.117 = f32[4,1024,2,128]{3,2,1,0:T(2,128)} reshape(f32[4096,256]{1,0:T(8,128)} %all-gather.15.cloned.1.call-done) | data formatting | bytes 8388608 | tf_op jit(solution)/shard_map/reshape | solution.py:122
  91.9 6.8 %copy.7 = f32[4,1024,2,128]{3,0,2,1:T(4,128)} copy(f32[4,1024,2,128]{3,2,1,0:T(2,128)} %reshape.117) | data formatting | bytes 8388608 | tf_op jit(solution)/shard_map/reshape | solution.py:122
  98.8 5.5 %reshape.118.block_ref = f32[1024,1024]{1,0:T(8,128)} reshape(f32[1024,2,4,128]{3,2,1,0:T(4,128)} %bitcast.14) | data formatting | bytes 8388608 | tf_op jit(solution)/shard_map/reshape | solution.py:123
  104.2 0.0 all-gather.11.cloned.1.call-update
  104.2 0.2 all-gather.13.cloned.1.call-start
  104.5 0.3 all-gather.13.cloned.1.call-update
  105.0 0.0 copy-start.2
  105.0 0.6 compare_reduce_fusion
  105.7 0.0 copy-start
  105.7 2.2 copy-done
  107.9 78.4 %shard_map.17 = f32[1024,1024]{1,0:T(8,128)S(1)} custom-call(f32[1024,1024]{1,0:T(8,128)S(1)} %copy-done), custom_call_target="tpu_custom_call" | custom-call | flops 64424509440 | bytes 8388608 | tf_op jit(solution)/shard_map/pallas_call | solution.py:84
  186.2 0.0 copy-done.2
  186.3 0.0 copy-start.1
  186.3 2.0 copy-done.1
  188.2 0.0 all-gather.11.cloned.1.call-done
  188.2 7.7 %reshape.119 = f32[4,1280,2,128]{3,2,1,0:T(2,128)} reshape(f32[5120,256]{1,0:T(8,128)} %all-gather.11.cloned.1.call-done) | data formatting | bytes 10485760 | tf_op jit(solution)/shard_map/reshape | solution.py:122
  196.0 8.8 %copy.5 = f32[1280,2,4,128]{0,3,2,1:T(8,128)} copy(f32[1280,2,4,128]{3,1,0,2:T(2,128)} %bitcast.13) | data formatting | bytes 10485760 | tf_op jit(solution)/shard_map/transpose | solution.py:123
  204.8 0.0 slice-start
  204.8 13.3 %fusion.25 = f32[1280,1024]{1,0:T(8,128)} fusion(f32[1280,1024]{0,1:T(8,128)} %bitcast.15, f32[1024,1024]{1,0:T(8,128)} %copy-done.1), kind=kOutput, calls=%fused_computation.42 | convolution fusion | flops 8053063680 | bytes 14680064 | tf_op jit(solution)/shard_map/dot_general | solution.py:135
  218.1 2.1 fusion.1
  220.3 44.4 %all-gather.13.cloned.1.call-done = f32[1024,2560]{1,0:T(8,128)} async-done(((f32[128,2560]{1,0:T(8,128)}), f32[1024,2560]{1,0:T(8,128)}) %all-gather.13.cloned.1.call-update) | async-done | bytes 10485776 | tf_op jit(solution)/shard_map/all_gather | solution.py:117
  264.6 0.0 slice-done
  264.6 3.0 %fusion = f32[1024,2560]{1,0:T(8,128)} fusion(f32[1024,2560]{1,0:T(8,128)} %all-gather.13.cloned.1.call-done, s32[256]{0:T(256)S(1)} %slice-done, pred[256]{0:T(512)(128)(4,1)S(1)} %slice.77, pred[]{:T(512)} %compare_reduce_fusion), kind=kLoop, calls=%fused_computation.3 | loop fusion | flops 1048576 | bytes 2098944 | tf_op jit(solution)/shard_map/scatter | solution.py:148
  267.7 27.6 %convolution_subtract_fusion = f32[1280,2560]{1,0:T(8,128)} fusion(f32[1280,1024]{1,0:T(8,128)} %fusion.1, f32[1024,2560]{1,0:T(8,128)} %fusion, f32[1280,2560]{1,0:T(8,128)} %param.5, pred[2560]{0:T(1024)(128)(4,1)S(1)} %broadcast_compare_fusion, pred[1280]{0:T(1024)(128)(4,1)S(1)} %broadcast_compare_fusion.1), kind=kOutput, calls=%fused_computation | convolution fusion | flops 20142489600 | bytes 41946880 | tf_op jit(solution)/shard_map/dot_general | solution.py:150
  (7 shorter events, 0.1 us)
Async XLA Ops:
  6.5 26.3 %all-gather.9.cloned.1.call-start = ((), (), s32[]{:S(2)}) async-start(), calls=%async_computation | async-start | bytes 1179648 | tf_op jit(solution)/shard_map/all_gather | solution.py:117
  8.1 78.1 %all-gather.15.cloned.1.call-start = ((), (), s32[]{:S(2)}) async-start(), calls=%async_computation.3 | async-start | bytes 5242880 | tf_op jit(solution)/shard_map/all_gather | solution.py:122
  32.8 155.4 %all-gather.11.cloned.1.call-start = ((), (), s32[]{:S(2)}) async-start(), calls=%async_computation.1 | async-start | bytes 6553600 | tf_op jit(solution)/shard_map/all_gather | solution.py:122
  104.2 160.4 %all-gather.13.cloned.1.call-start = ((), (), s32[]{:S(2)}) async-start(), calls=%async_computation.2 | async-start | bytes 11796480 | tf_op jit(solution)/shard_map/all_gather | solution.py:117
  105.0 81.2 %copy-start.2 = (s32[2560]{0:T(1024)}, s32[2560]{0:T(1024)S(1)}, u32[]{:S(2)}) copy-start(s32[2560]{0:T(1024)S(1)} %fusion.15) | copy-start | bytes 30724
  105.7 2.2 copy-start
  186.3 2.0 copy-start.1
  204.8 59.8 %slice-start = ((s32[2560]{0:T(1024)}), s32[256]{0:T(256)S(1)}, s32[]{:S(2)}) async-start(s32[2560]{0:T(1024)} %copy-done.2), calls=%async_computation.4 | async-start | bytes 2048 | tf_op jit(solution)/shard_map/slice | solution.py:146
Sparse Core Ops, SparseCore 0:
  8.9 23.8 all-gather.8
  34.7 51.4 all-gather.14
  104.4 61.3 all-gather.10
  167.3 97.2 all-gather.12

commit v2 on v1

v2 whole, which is shorter than its diff:
```python
import jax
import jax.numpy as jnp
from jax import lax
from jax.experimental import pallas as pl
from jax.experimental.pallas import tpu as pltpu
from jax.sharding import PartitionSpec as P

TILE = 128
PIVOT = 512
STEPS = 2
ALL = PIVOT * STEPS
SUB = 8
HIGHEST = lax.Precision.HIGHEST


def dot32(a, b):
    return jnp.dot(a, b, precision=HIGHEST, preferred_element_type=jnp.float32)


def invert_tile(tile):
    groups = TILE // SUB
    strips = [tile[g * SUB : (g + 1) * SUB, :] for g in range(groups)]
    shape = (SUB, TILE)
    lane = lax.broadcasted_iota(jnp.int32, shape, 1)
    sub = lax.broadcasted_iota(jnp.int32, shape, 0)

    def lanes(value, column):
        return jnp.broadcast_to(value[:, column : column + 1], shape)

    def subs(value, row):
        return jnp.broadcast_to(value[row : row + 1, :], shape)

    for g in range(groups):
        first = g * SUB
        panel = strips[g]
        columns = [lanes(panel, first + m) for m in range(SUB)]
        in_group = (lane >= first) & (lane < first + SUB)
        panel = jnp.where(in_group, jnp.where(lane - first == sub, 1.0, 0.0), panel)
        for m in range(SUB):
            own = sub == m
            scale = 1.0 / subs(columns[m], m)
            factor = jnp.where(own, 0.0, columns[m])
            row = subs(panel, m) * scale
            panel = jnp.where(own, row, panel - factor * row)
            for n in range(m + 1, SUB):
                there = subs(columns[n], m) * scale
                columns[n] = jnp.where(own, there, columns[n] - factor * there)
        strips[g] = panel
        rows = [subs(panel, m) for m in range(SUB)]
        for i in range(groups):
            if i == g:
                continue
            value = strips[i]
            total = jnp.where(in_group, 0.0, value)
            for m in range(SUB):
                total = total - lanes(value, first + m) * rows[m]
            strips[i] = total
    return jnp.concatenate(strips, axis=0)


def split3(value):
    high = value.astype(jnp.bfloat16)
    rest = value - high.astype(jnp.float32)
    middle = rest.astype(jnp.bfloat16)
    low = (rest - middle.astype(jnp.float32)).astype(jnp.bfloat16)
    return high, middle, low


def split2(value):
    high = value.astype(jnp.bfloat16)
    return high, (value - high.astype(jnp.float32)).astype(jnp.bfloat16)


def widen_left(value):
    high, middle, low = split3(value)
    return jnp.concatenate([high, high, middle, high, low, middle], axis=1)


def widen_right(value):
    high, middle, low = split3(value)
    return jnp.concatenate([high, middle, high, low, high, middle], axis=0)


def dot16(a, b):
    return jnp.dot(a, b, preferred_element_type=jnp.float32)


def invert_in_place(work, wide_col, wide_row):
    majors, minors, _, size = work.shape
    count = majors * minors

    def step(t, carry):
        major, minor = t // minors, t % minors
        at = pl.ds(pl.multiple_of(t * TILE, TILE), TILE)
        inverse = invert_tile(work[major, minor, :, at])
        row = dot32(inverse, work[major, minor, :, :])
        wide_col[...] = widen_left(work[:, :, :, at].reshape(count * TILE, TILE))
        work[major, minor, :, :] = row
        work[major, minor, :, at] = inverse
        row = work[major, minor, :, :]
        wide_row[...] = widen_right(row)
        work[:, :, :, at] = jnp.zeros((majors, minors, TILE, TILE), jnp.float32)
        for i in range(majors):
            left = wide_col[i * minors * TILE : (i + 1) * minors * TILE, :]
            change = dot16(left, wide_row[...]).reshape(minors, TILE, size)
            work[i] = work[i] - change
        work[major, minor, :, :] = row
        return carry

    lax.fori_loop(0, count, step, 0)


def inverse_kernel(block_ref, out_ref, wide_col, wide_row):
    out_ref[...] = block_ref[...]
    invert_in_place(out_ref, wide_col, wide_row)


def wide_scratch(size):
    return [
        pltpu.VMEM((size, 6 * TILE), jnp.bfloat16),
        pltpu.VMEM((6 * TILE, size), jnp.bfloat16),
    ]


def spd_inverse(block):
    size = block.shape[0]
    shape = (size // (2 * TILE), 2, TILE, size)
    out = pl.pallas_call(
        inverse_kernel,
        out_shape=jax.ShapeDtypeStruct(shape, jnp.float32),
        in_specs=[pl.BlockSpec(memory_space=pltpu.VMEM)],
        out_specs=pl.BlockSpec(memory_space=pltpu.VMEM),
        scratch_shapes=wide_scratch(size),
        compiler_params=pltpu.CompilerParams(vmem_limit_bytes=32 << 20),
        cost_estimate=pl.CostEstimate(
            flops=60 * size**3, bytes_accessed=8 * size * size, transcendentals=0
        ),
    )(block.reshape(shape))
    return out.reshape(size, size)


def gain_kernel(
    rows_count,
    cols_count,
    factor_ref,
    gain_high,
    gain_low,
    work,
    panel,
    wide_col,
    wide_row,
    high_ref,
    low_ref,
    local_sem,
    line_send,
    line_recv,
    plane_send,
    plane_recv,
    pair_send,
    pair_recv,
    panel_send,
    panel_recv,
):
    majors = rows_count // 2
    slots = ALL // (TILE * cols_count)
    r = lax.axis_index("row")
    c = lax.axis_index("col")
    major, minor = r // 2, r % 2
    mesh_id = pl.DeviceIdType.MESH
    pair = (major * 2 + 1 - minor, c)
    line = [(lax.rem(major + j, majors) * 2 + minor, c) for j in range(1, majors)]
    plane = [(r, lax.rem(c + j, cols_count)) for j in range(1, cols_count)]
    sources = [lax.rem(c + cols_count - j, cols_count) for j in range(cols_count)]

    barrier = pltpu.get_barrier_semaphore()
    for device in [pair] + line + plane:
        pl.semaphore_signal(barrier, inc=1, device_id=device, device_id_type=mesh_id)

    def place(slot, owner):
        return pl.ds(pl.multiple_of((slot * cols_count + owner) * TILE, TILE), TILE)

    def tile_of(slot):
        return factor_ref.at[pl.ds(0, TILE), pl.ds(slot * TILE, TILE)]

    own = []
    for s in range(slots):
        copy = pltpu.make_async_copy(
            tile_of(s), work.at[major, minor, :, place(s, c)], local_sem.at[s]
        )
        copy.start()
        own.append(copy)
    own_panel = pltpu.make_async_copy(
        factor_ref.at[:, pl.ds(0, slots * TILE)], panel.at[c], local_sem.at[slots]
    )
    own_panel.start()
    pl.semaphore_wait(barrier, 1 + len(line) + len(plane))

    line_copies = []
    for j, device in enumerate(line):
        for s in range(slots):
            copy = pltpu.make_async_remote_copy(
                src_ref=tile_of(s),
                dst_ref=work.at[major, minor, :, place(s, c)],
                send_sem=line_send.at[j, s],
                recv_sem=line_recv.at[j, s],
                device_id=device,
                device_id_type=mesh_id,
            )
            copy.start()
            line_copies.append(copy)

    def group(s, owner):
        return work.at[:, minor, :, place(s, owner)]

    def pair_group(j):
        copies = []
        for s in range(slots):
            copy = pltpu.make_async_remote_copy(
                src_ref=group(s, sources[j]),
                dst_ref=group(s, sources[j]),
                send_sem=pair_send.at[j, s],
                recv_sem=pair_recv.at[j, s],
                device_id=pair,
                device_id_type=mesh_id,
            )
            copy.start()
            copies.append(copy)
        return copies

    for copy in own:
        copy.wait()
    for copy in line_copies:
        copy.wait_recv()
    plane_copies = []
    for j, device in enumerate(plane):
        copies = []
        for s in range(slots):
            copy = pltpu.make_async_remote_copy(
                src_ref=group(s, c),
                dst_ref=group(s, c),
                send_sem=plane_send.at[j, s],
                recv_sem=plane_recv.at[j, s],
                device_id=device,
                device_id_type=mesh_id,
            )
            copy.start()
            copies.append(copy)
        plane_copies.append(copies)
    pair_copies = pair_group(0)
    for j, copies in enumerate(plane_copies):
        for copy in copies:
            copy.wait_recv()
        pair_copies += pair_group(j + 1)
    panel_copies = []
    for j, device in enumerate(plane):
        copy = pltpu.make_async_remote_copy(
            src_ref=factor_ref.at[:, pl.ds(0, slots * TILE)],
            dst_ref=panel.at[c],
            send_sem=panel_send.at[j],
            recv_sem=panel_recv.at[j],
            device_id=device,
            device_id_type=mesh_id,
        )
        copy.start()
        panel_copies.append(copy)
    for copies in plane_copies:
        for copy in copies:
            copy.wait_send()
    for copy in pair_copies:
        copy.wait()
    for copy in line_copies:
        copy.wait_send()

    invert_in_place(work, wide_col, wide_row)

    own_panel.wait()
    for copy in panel_copies:
        copy.wait()
    size = work.shape[-1]
    for i in range(majors):
        value = work[i].reshape(2 * TILE, size)
        rows = pl.ds(i * 2 * TILE, 2 * TILE)
        high_ref[rows, :], low_ref[rows, :] = split2(value)
    chunk = 2 * TILE
    half = size // 2

    @pl.loop(0, gain_high.shape[0] // chunk)
    def _(i):
        rows = pl.ds(pl.multiple_of(i * chunk, chunk), chunk)
        parts = [
            panel[owner, rows, s * TILE : (s + 1) * TILE]
            for s in range(slots)
            for owner in range(cols_count)
        ]
        left = jnp.concatenate(parts, axis=1)
        high, low = split2(left)
        for n in range(2):
            cols = slice(n * half, (n + 1) * half)
            gain = (
                dot16(high, high_ref[:, cols])
                + dot16(high, low_ref[:, cols])
                + dot16(low, high_ref[:, cols])
            )
            gain_high[rows, cols], gain_low[rows, cols] = split2(gain)

    gain_high[0:TILE, :], gain_low[0:TILE, :] = split2(-work[major, minor, :, :])


def gathered_gain(factor, rows_count, cols_count):
    height = factor.shape[0]
    majors = rows_count // 2
    slots = ALL // (TILE * cols_count)
    dma = pltpu.SemaphoreType.DMA
    return pl.pallas_call(
        lambda *refs: gain_kernel(rows_count, cols_count, *refs),
        out_shape=[jax.ShapeDtypeStruct((height, ALL), jnp.bfloat16)] * 2,
        in_specs=[pl.BlockSpec(memory_space=pl.ANY)],
        out_specs=[pl.BlockSpec(memory_space=pltpu.VMEM)] * 2,
        scratch_shapes=[
            pltpu.VMEM((majors, 2, TILE, ALL), jnp.float32),
            pltpu.VMEM((cols_count, height, slots * TILE), jnp.float32),
        ]
        + wide_scratch(ALL)
        + [
            pltpu.VMEM((ALL, ALL), jnp.bfloat16),
            pltpu.VMEM((ALL, ALL), jnp.bfloat16),
            dma((slots + 1,)),
            dma((majors - 1, slots)),
            dma((majors - 1, slots)),
            dma((cols_count - 1, slots)),
            dma((cols_count - 1, slots)),
            dma((cols_count, slots)),
            dma((cols_count, slots)),
            dma((cols_count - 1,)),
            dma((cols_count - 1,)),
        ],
        compiler_params=pltpu.CompilerParams(
            collective_id=0, has_side_effects=True, vmem_limit_bytes=40 << 20
        ),
        cost_estimate=pl.CostEstimate(
            flops=60 * ALL**3, bytes_accessed=8 * ALL * ALL, transcendentals=0
        ),
    )(factor)


def largest(extent, limit):
    return max(n for n in range(TILE, limit + 1, TILE) if extent % n == 0)


def update_kernel(
    rows_count, cols_count, gain_high, gain_low, rows_ref, base_ref, out_ref, high_ref, low_ref
):
    j, i = pl.program_id(0), pl.program_id(1)
    tall, wide = out_ref.shape
    tiles = ALL // TILE
    col_tiles = [
        (j * (wide // TILE) + n) * cols_count + lax.axis_index("col") for n in range(wide // TILE)
    ]
    row_tiles = [
        (i * (tall // TILE) + n) * rows_count + lax.axis_index("row") for n in range(tall // TILE)
    ]

    @pl.when(i == 0)
    def _():
        high_ref[...], low_ref[...] = split2(rows_ref[...])

        for n, tile in enumerate(col_tiles):

            @pl.when(tile < tiles)
            def _(n=n, tile=tile):
                cols = slice(n * TILE, (n + 1) * TILE)
                down = lax.broadcasted_iota(jnp.int32, (ALL, TILE), 0)
                across = lax.broadcasted_iota(jnp.int32, (ALL, TILE), 1)
                marks = jnp.where(down - across == tile * TILE, 1.0, 0.0)
                high_ref[:, cols] = marks.astype(jnp.bfloat16)
                low_ref[:, cols] = jnp.zeros((ALL, TILE), jnp.bfloat16)

    rows = pl.ds(pl.multiple_of(i * tall, tall), tall)
    high, low = gain_high[rows, :], gain_low[rows, :]
    change = (
        dot16(high, high_ref[...]) + dot16(high, low_ref[...]) + dot16(low, high_ref[...])
    )
    out_ref[...] = base_ref[...] - change

    for m, row_tile in enumerate(row_tiles):
        for n, col_tile in enumerate(col_tiles):

            @pl.when((row_tile < tiles) | (col_tile < tiles))
            def _(m=m, n=n):
                part = (slice(m * TILE, (m + 1) * TILE), slice(n * TILE, (n + 1) * TILE))
                out_ref[part] = -change[part]


def update(gain_high, gain_low, pivot_rows, factor, rows_count, cols_count):
    height, width = factor.shape
    tall, wide = largest(height, 2 * TILE), largest(width, 5 * TILE)
    whole = pl.BlockSpec(gain_high.shape, lambda j, i: (0, 0), pipeline_mode=pl.Buffered(1))
    block = pl.BlockSpec((tall, wide), lambda j, i: (i, j))
    return pl.pallas_call(
        lambda *refs: update_kernel(rows_count, cols_count, *refs),
        out_shape=jax.ShapeDtypeStruct(factor.shape, jnp.float32),
        grid=(width // wide, height // tall),
        in_specs=[whole, whole, pl.BlockSpec((ALL, wide), lambda j, i: (0, j)), block],
        out_specs=block,
        scratch_shapes=[pltpu.VMEM((ALL, wide), jnp.bfloat16)] * 2,
        compiler_params=pltpu.CompilerParams(vmem_limit_bytes=40 << 20),
        cost_estimate=pl.CostEstimate(
            flops=6 * height * width * ALL, bytes_accessed=12 * height * width, transcendentals=0
        ),
    )(gain_high, gain_low, pivot_rows, factor)


def per_device(factor):
    rows_count = lax.axis_size("row")
    cols_count = lax.axis_size("col")
    row_place = lax.axis_index("row")
    tiles = ALL // TILE
    row_slots = -(-tiles // rows_count)
    col_slots = -(-tiles // cols_count)
    def gather_rows(value):
        width = value.shape[1]
        got = lax.all_gather(value, "row").reshape(rows_count, row_slots, TILE, width)
        return got.transpose(1, 0, 2, 3).reshape(-1, width)[:ALL]

    def gather_cols(value):
        height = value.shape[0]
        got = lax.all_gather(value, "col").reshape(cols_count, height, col_slots, TILE)
        return got.transpose(1, 2, 0, 3).reshape(height, -1)[:, :ALL]

    if rows_count == tiles and cols_count > 1 and tiles % cols_count == 0:
        pivot_rows = gather_rows(factor[:TILE, :])
        gain_high, gain_low = gathered_gain(factor, rows_count, cols_count)
    else:
        row_slab = factor[: row_slots * TILE, :]
        col_slab = factor[:, : col_slots * TILE]
        pivot_block = gather_cols(gather_rows(factor[: row_slots * TILE, : col_slots * TILE]))
        pivot_block, row_slab, col_slab = lax.optimization_barrier(
            (pivot_block, row_slab, col_slab)
        )
        pivot_rows = gather_rows(row_slab)
        pivot_cols = gather_cols(col_slab)
        inverse = spd_inverse(pivot_block)
        gain = jnp.dot(
            pivot_cols, inverse, precision=lax.Precision.HIGH, preferred_element_type=jnp.float32
        )
        for s in range(row_slots):
            own = s * rows_count + row_place
            start = jnp.minimum(own, tiles - 1) * TILE
            head = gain[s * TILE : (s + 1) * TILE]
            head = jnp.where(own < tiles, -lax.dynamic_slice(inverse, (start, 0), head.shape), head)
            gain = gain.at[s * TILE : (s + 1) * TILE].set(head)
        gain_high = lax.reduce_precision(gain, 8, 7)
        gain_low = (gain - gain_high).astype(jnp.bfloat16)
        gain_high = gain_high.astype(jnp.bfloat16)
    return update(gain_high, gain_low, pivot_rows, factor, rows_count, cols_count)


def solution(mesh):
    placed = (P("row", "col"),)
    return jax.shard_map(
        per_device, mesh=mesh, in_specs=placed, out_specs=P("row", "col"), check_vma=False
    )
```

time: 306 us -> 201 us (0.66); the launches traced: 302 us -> 201 us
  waiting for transfers between devices: 118 us -> 0.02 us
  Pallas kernels: 78.4 us -> 182 us
  matrix products: 41 us -> 0 us
  local copies, waits for them, and re-layouts: 45.3 us -> 5.7 us
  other arithmetic: 5.86 us -> 0 us
    pallas_call x1 -> x2, Pallas kernels: 78.4 us -> 182 us  [the longest x1 145 us: gathered_gain(): pl.pallas_call(lambda *refs: gain_kernel(rows_count, cols_count, *refs),...]
    all_gather x2 -> x1, waiting for transfers between devices: 69 us -> 0.01 us  [gather_rows(): lax.all_gather(value, 'row').reshape(rows_count, row_slots, TILE, width)]
    all_gather x2 -> x0, waiting for transfers between devices: 48.3 us -> none  [gather_cols(): lax.all_gather(value, 'col').reshape(cols_count, height, col_slots, TILE)]
    dot_general x2 -> x0, matrix products: 41 us -> none  [the longest x1 27.6 us: per_device(): jnp.dot(gain, pivot_rows, precision=lax.Precision.HIGH, preferred_element...]
    reshape x4 -> x0, local copies, waits for them, and re-layouts: 25.8 us -> none  [the longest x3 20.3 us: gather_cols(): lax.all_gather(value, 'col').reshape(cols_count, height, col_slots, TILE)]
    transpose x1 -> x0, local copies, waits for them, and re-layouts: 8.82 us -> none  [gather_cols(): return got.transpose(1, 2, 0, 3).reshape(height, -1)[:, :ALL]]
    scatter x2 -> x0, other arithmetic: 5.17 us -> none  [the longest x1 3.05 us: per_device(): pivot_rows = pivot_rows.at[:, :width].set(lead)]
    slice x7 -> x1, local copies, waits for them, and re-layouts: 6.6 us -> 2.48 us  [per_device(): pivot_rows = gather_rows(factor[:TILE, :])]
  transfers between devices with their start and end apart: 4 -> 1, of which waited for: 3 -> 0; matrix products, arithmetic and copies ran while one was open for 13% -> 0% of each run, Pallas kernels for 26% -> 72%
where the time goes in v2:
time: 201 us
  Pallas kernels  182 us (91%)
  between operations  13.4 us (7%)
  local copies, waits for them, and re-layouts  5.7 us (3%)
    pallas_call x1, Pallas kernels, gathered_gain(): pl.pallas_call(lambda *refs: gain_kernel(rows_count, cols_count, *refs),...  145 us
    pallas_call x1, Pallas kernels, update(): pl.pallas_call(lambda *refs: update_kernel(rows_count, cols_count, *refs)...  36.2 us
  transfers between devices with their start and end apart: 1, of which 0 were waited for; matrix products, arithmetic and copies ran while one was open for 0% of the time, Pallas kernels for 72%

profile of v2, /device:TPU:13, one launch (start us, length us, event | category | flops | bytes accessed | tf_op | source)
XLA Modules:
  0.0 200.7 jit_solution(8459933785903002599)
XLA Ops:
  6.5 0.0 all-gather.3.cloned.1.call-start
  6.5 2.5 %slice.3 = f32[128,2560]{1,0:T(8,128)} slice(f32[1280,2560]{1,0:T(8,128)} %refs_3_.1), slice={[0:128], [0:2560]} | slice | bytes 2621440 | tf_op jit(solution)/shard_map/slice | solution.py:431
  9.0 0.0 all-gather.3.cloned.1.call-update
  9.0 145.4 %shard_map.17 = (bf16[1280,1024]{1,0:T(8,128)(2,1)S(1)}, bf16[1280,1024]{1,0:T(8,128)(2,1)S(1)}) custom-call(f32[1280,2560]{1,0:T(8,128)} %refs_3_.1), custom_call_target="tpu_custom_call" | custom-call | flops 64424509440 | bytes 8388608 | tf_op jit(solution)/shard_map/pallas_call | solution.py:314
  154.4 0.0 copy-start
  154.4 1.5 copy-done
  155.9 0.0 all-gather.3.cloned.1.call-done.refs_2_
  155.9 0.0 copy-start.1
  155.9 1.7 copy-done.1
  157.7 36.2 %shard_map.18 = f32[1280,2560]{1,0:T(8,128)} custom-call(bf16[1280,1024]{1,0:T(8,128)(2,1)S(1)} %get-tuple-element.7.refs_0_, bf16[1280,1024]{1,0:T(8,128)(2,1)S(1)} %copy-done.1, f32[1024,2560]{1,0:T(8,128)} %all-gather.3.cloned.1.call-done.refs_2_, f32[1280,2560]{1,0:T(8,128)} %refs_3_.1), custom_call_target="tpu_custom_call" | custom-call | flops 20132659200 | bytes 39321600 | tf_op jit(solution)/shard_map/pallas_call | solution.py:399
Async XLA Ops:
  6.5 149.4 %all-gather.3.cloned.1.call-start = ((), (), s32[]{:S(2)}) async-start(), calls=%async_computation | async-start | bytes 11796480 | tf_op jit(solution)/shard_map/all_gather | solution.py:422
  154.4 1.5 copy-start
  155.9 1.7 copy-start.1
Sparse Core Ops, SparseCore 0:
  9.2 99.8 all-gather.2

commit v3 on v2

--- a/solution.py
+++ b/solution.py
@@ -85,7 +85,7 @@
     return jnp.dot(a, b, preferred_element_type=jnp.float32)
 
 
-def invert_in_place(work, wide_col, wide_row):
+def invert_in_place(work, wide_col, wide_row, first, last):
     majors, minors, _, size = work.shape
     count = majors * minors
 
@@ -107,12 +107,12 @@
         work[major, minor, :, :] = row
         return carry
 
-    lax.fori_loop(0, count, step, 0)
+    lax.fori_loop(first, last, step, 0)
 
 
 def inverse_kernel(block_ref, out_ref, wide_col, wide_row):
     out_ref[...] = block_ref[...]
-    invert_in_place(out_ref, wide_col, wide_row)
+    invert_in_place(out_ref, wide_col, wide_row, 0, out_ref.shape[0] * out_ref.shape[1])
 
 
 def wide_scratch(size):
@@ -160,6 +160,7 @@
     pair_recv,
     panel_send,
     panel_recv,
+    ready,
 ):
     majors = rows_count // 2
     slots = ALL // (TILE * cols_count)
@@ -197,6 +198,7 @@
 
     line_copies = []
     for j, device in enumerate(line):
+        copies = []
         for s in range(slots):
             copy = pltpu.make_async_remote_copy(
                 src_ref=tile_of(s),
@@ -207,17 +209,37 @@
                 device_id_type=mesh_id,
             )
             copy.start()
-            line_copies.append(copy)
-
-    def group(s, owner):
-        return work.at[:, minor, :, place(s, owner)]
+            copies.append(copy)
+        line_copies.append(copies)
+
+    plane_copies = [[] for _ in plane]
+    for j in range(majors):
+        source = lax.rem(major + majors - j, majors)
+        for copy in line_copies[j - 1] if j else own:
+            if j:
+                copy.wait_recv()
+            else:
+                copy.wait()
+        for p, device in enumerate(plane):
+            for s in range(slots):
+                copy = pltpu.make_async_remote_copy(
+                    src_ref=work.at[source, minor, :, place(s, c)],
+                    dst_ref=work.at[source, minor, :, place(s, c)],
+                    send_sem=plane_send.at[j, p, s],
+                    recv_sem=plane_recv.at[j, p, s],
+                    device_id=device,
+                    device_id_type=mesh_id,
+                )
+                copy.start()
+                plane_copies[p].append(copy)
 
     def pair_group(j):
         copies = []
         for s in range(slots):
+            group = work.at[:, minor, :, place(s, sources[j])]
             copy = pltpu.make_async_remote_copy(
-                src_ref=group(s, sources[j]),
-                dst_ref=group(s, sources[j]),
+                src_ref=group,
+                dst_ref=group,
                 send_sem=pair_send.at[j, s],
                 recv_sem=pair_recv.at[j, s],
                 device_id=pair,
@@ -227,30 +249,22 @@
             copies.append(copy)
         return copies
 
-    for copy in own:
-        copy.wait()
-    for copy in line_copies:
-        copy.wait_recv()
-    plane_copies = []
-    for j, device in enumerate(plane):
-        copies = []
-        for s in range(slots):
-            copy = pltpu.make_async_remote_copy(
-                src_ref=group(s, c),
-                dst_ref=group(s, c),
-                send_sem=plane_send.at[j, s],
-                recv_sem=plane_recv.at[j, s],
-                device_id=device,
-                device_id_type=mesh_id,
-            )
-            copy.start()
-            copies.append(copy)
-        plane_copies.append(copies)
     pair_copies = pair_group(0)
-    for j, copies in enumerate(plane_copies):
+    for p, copies in enumerate(plane_copies):
         for copy in copies:
             copy.wait_recv()
-        pair_copies += pair_group(j + 1)
+        pair_copies += pair_group(p + 1)
+    for device in plane:
+        pl.semaphore_signal(ready, inc=1, device_id=device, device_id_type=mesh_id)
+    for copies in plane_copies + line_copies:
+        for copy in copies:
+            copy.wait_send()
+    for copy in pair_copies:
+        copy.wait()
+
+    invert_in_place(work, wide_col, wide_row, 0, 1)
+
+    pl.semaphore_wait(ready, len(plane))
     panel_copies = []
     for j, device in enumerate(plane):
         copy = pltpu.make_async_remote_copy(
@@ -263,15 +277,8 @@
         )
         copy.start()
         panel_copies.append(copy)
-    for copies in plane_copies:
-        for copy in copies:
-            copy.wait_send()
-    for copy in pair_copies:
-        copy.wait()
-    for copy in line_copies:
-        copy.wait_send()
-
-    invert_in_place(work, wide_col, wide_row)
+
+    invert_in_place(work, wide_col, wide_row, 1, majors * 2)
 
     own_panel.wait()
     for copy in panel_copies:
@@ -327,12 +334,13 @@
             dma((slots + 1,)),
             dma((majors - 1, slots)),
             dma((majors - 1, slots)),
-            dma((cols_count - 1, slots)),
-            dma((cols_count - 1, slots)),
+            dma((majors, cols_count - 1, slots)),
+            dma((majors, cols_count - 1, slots)),
             dma((cols_count, slots)),
             dma((cols_count, slots)),
             dma((cols_count - 1,)),
             dma((cols_count - 1,)),
+            pltpu.SemaphoreType.REGULAR,
         ],
         compiler_params=pltpu.CompilerParams(
             collective_id=0, has_side_effects=True, vmem_limit_bytes=40 << 20
@@ -348,7 +356,7 @@
 
 
 def update_kernel(
-    rows_count, cols_count, gain_high, gain_low, rows_ref, base_ref, out_ref, high_ref, low_ref
+    rows_count, cols_count, gain_high, gain_low, rows_ref, base_ref, out_ref, wide_ref
 ):
     j, i = pl.program_id(0), pl.program_id(1)
     tall, wide = out_ref.shape
@@ -362,7 +370,10 @@
 
     @pl.when(i == 0)
     def _():
-        high_ref[...], low_ref[...] = split2(rows_ref[...])
+        high, low = split2(rows_ref[...])
+        wide_ref[0:ALL, :] = high
+        wide_ref[ALL : 2 * ALL, :] = low
+        wide_ref[2 * ALL : 3 * ALL, :] = high
 
         for n, tile in enumerate(col_tiles):
 
@@ -371,15 +382,14 @@
                 cols = slice(n * TILE, (n + 1) * TILE)
                 down = lax.broadcasted_iota(jnp.int32, (ALL, TILE), 0)
                 across = lax.broadcasted_iota(jnp.int32, (ALL, TILE), 1)
-                marks = jnp.where(down - across == tile * TILE, 1.0, 0.0)
-                high_ref[:, cols] = marks.astype(jnp.bfloat16)
-                low_ref[:, cols] = jnp.zeros((ALL, TILE), jnp.bfloat16)
+                marks = jnp.where(down - across == tile * TILE, 1.0, 0.0).astype(jnp.bfloat16)
+                wide_ref[0:ALL, cols] = marks
+                wide_ref[ALL : 2 * ALL, cols] = jnp.zeros((ALL, TILE), jnp.bfloat16)
+                wide_ref[2 * ALL : 3 * ALL, cols] = marks
 
     rows = pl.ds(pl.multiple_of(i * tall, tall), tall)
     high, low = gain_high[rows, :], gain_low[rows, :]
-    change = (
-        dot16(high, high_ref[...]) + dot16(high, low_ref[...]) + dot16(low, high_ref[...])
-    )
+    change = dot16(jnp.concatenate([high, high, low], axis=1), wide_ref[...])
     out_ref[...] = base_ref[...] - change
 
     for m, row_tile in enumerate(row_tiles):
@@ -393,7 +403,7 @@
 
 def update(gain_high, gain_low, pivot_rows, factor, rows_count, cols_count):
     height, width = factor.shape
-    tall, wide = largest(height, 2 * TILE), largest(width, 5 * TILE)
+    tall, wide = largest(height, 5 * TILE), largest(width, 5 * TILE)
     whole = pl.BlockSpec(gain_high.shape, lambda j, i: (0, 0), pipeline_mode=pl.Buffered(1))
     block = pl.BlockSpec((tall, wide), lambda j, i: (i, j))
     return pl.pallas_call(
@@ -402,7 +412,7 @@
         grid=(width // wide, height // tall),
         in_specs=[whole, whole, pl.BlockSpec((ALL, wide), lambda j, i: (0, j)), block],
         out_specs=block,
-        scratch_shapes=[pltpu.VMEM((ALL, wide), jnp.bfloat16)] * 2,
+        scratch_shapes=[pltpu.VMEM((3 * ALL, wide), jnp.bfloat16)],
         compiler_params=pltpu.CompilerParams(vmem_limit_bytes=40 << 20),
         cost_estimate=pl.CostEstimate(
             flops=6 * height * width * ALL, bytes_accessed=12 * height * width, transcendentals=0

time: 201 us -> 165 us (0.82); the launches traced: 201 us -> 162 us
  Pallas kernels: 182 us -> 143 us
    pallas_call x1, Pallas kernels: 145 us -> 110 us  [gathered_gain(): pl.pallas_call(lambda *refs: gain_kernel(rows_count, cols_count, *refs),...]
    pallas_call x1, Pallas kernels: 36.2 us -> 32.4 us  [update(): pl.pallas_call(lambda *refs: update_kernel(rows_count, cols_count, *refs)...]
  transfers between devices with their start and end apart: 1 -> 1, of which waited for: 0 -> 0; matrix products, arithmetic and copies ran while one was open for 0% -> 0% of each run, Pallas kernels for 72% -> 68%
where the time goes in v3:
time: 165 us; the launch traced here: 162 us
  Pallas kernels  143 us (87%)
  between operations  13.4 us (8%)
  local copies, waits for them, and re-layouts  5.7 us (3%)
    pallas_call x1, Pallas kernels, gathered_gain(): pl.pallas_call(lambda *refs: gain_kernel(rows_count, cols_count, *refs),...  110 us
    pallas_call x1, Pallas kernels, update(): pl.pallas_call(lambda *refs: update_kernel(rows_count, cols_count, *refs)...  32.4 us
  transfers between devices with their start and end apart: 1, of which 0 were waited for; matrix products, arithmetic and copies ran while one was open for 0% of the time, Pallas kernels for 68%

profile of v3, /device:TPU:13, one launch (start us, length us, event | category | flops | bytes accessed | tf_op | source)
XLA Modules:
  0.0 161.9 jit_solution(4409407895290493013)
XLA Ops:
  6.5 0.0 all-gather.3.cloned.1.call-start
  6.5 2.5 %slice.3 = f32[128,2560]{1,0:T(8,128)} slice(f32[1280,2560]{1,0:T(8,128)} %refs_3_.1), slice={[0:128], [0:2560]} | slice | bytes 2621440 | tf_op jit(solution)/shard_map/slice | solution.py:441
  9.0 0.0 all-gather.3.cloned.1.call-update
  9.0 110.3 %shard_map.17 = (bf16[1280,1024]{1,0:T(8,128)(2,1)S(1)}, bf16[1280,1024]{1,0:T(8,128)(2,1)S(1)}) custom-call(f32[1280,2560]{1,0:T(8,128)} %refs_3_.1), custom_call_target="tpu_custom_call" | custom-call | flops 64424509440 | bytes 8388608 | tf_op jit(solution)/shard_map/pallas_call | solution.py:321
  119.4 0.0 copy-start
  119.4 1.5 copy-done
  120.9 0.0 all-gather.3.cloned.1.call-done.refs_2_
  120.9 0.0 copy-start.1
  120.9 1.7 %copy-done.1 = bf16[1280,1024]{1,0:T(8,128)(2,1)S(1)} copy-done((bf16[1280,1024]{1,0:T(8,128)(2,1)S(1)}, bf16[1280,1024]{1,0:T(8,128)(2,1)}, u32[]{:S(2)}) %copy-start.1) | copy-done | bytes 2621464
  122.6 32.4 %shard_map.18 = f32[1280,2560]{1,0:T(8,128)} custom-call(bf16[1280,1024]{1,0:T(8,128)(2,1)S(1)} %get-tuple-element.7.refs_0_, bf16[1280,1024]{1,0:T(8,128)(2,1)S(1)} %copy-done.1, f32[1024,2560]{1,0:T(8,128)} %all-gather.3.cloned.1.call-done.refs_2_, f32[1280,2560]{1,0:T(8,128)} %refs_3_.1), custom_call_target="tpu_custom_call" | custom-call | flops 20132659200 | bytes 39321600 | tf_op jit(solution)/shard_map/pallas_call | solution.py:409
Async XLA Ops:
  6.5 114.3 %all-gather.3.cloned.1.call-start = ((), (), s32[]{:S(2)}) async-start(), calls=%async_computation | async-start | bytes 11796480 | tf_op jit(solution)/shard_map/all_gather | solution.py:432
  119.4 1.5 copy-start
  120.9 1.7 %copy-start.1 = (bf16[1280,1024]{1,0:T(8,128)(2,1)S(1)}, bf16[1280,1024]{1,0:T(8,128)(2,1)}, u32[]{:S(2)}) copy-start(bf16[1280,1024]{1,0:T(8,128)(2,1)} %copy-done) | copy-start | bytes 7864324
Sparse Core Ops, SparseCore 0:
  9.2 99.8 all-gather.2
